TPU v7x, 128 devices: a whole 4x4x4 slice. The times are simulated.
128 devices in a mesh: row: 8 (over z, core), col: 16 (over x, y).
Axes of the slice: x: 4, y: 4, z: 4, core: 2. Of those that a mesh axis runs over, the one named last changes fastest.
Arguments:
- hessian_inverse: float32 [12288, 12288], P('row', 'col'), as said below
- weight: bfloat16 [12288, 4096], P('row', 'col'), may hold values from -6 to 6
- pruned: int32 [2, 512], replicated, may hold values from 0 to 12287, as said below
Outputs:
- hessian_after: float32 [12288, 12288], P('row', 'col')
- weight_after: bfloat16 [12288, 4096], P('row', 'col')
Inputs may be any that keep to these rules, and one draw needn't show every extreme that they name: `hessian_inverse`: symmetric and positive definite. `pruned`: all 1024 channel numbers are distinct.
All inputs are finite; a program needn't handle non-finite values.
Results may differ from a plain program's by a relative error of at most 0.001.
Values sent between devices are 32-bit elements; how exact they have to be, the bound alone decides.
No kernel may reach another device: no remote copies, remote signals or barrier semaphores. Data moves between devices by JAX's collectives and lax.ppermute only.
A program may use at most 128 MiB of HBM per device.

v0:
```python
import jax
import jax.numpy as jnp
from jax import lax
from jax.sharding import PartitionSpec as P

PANELS = 2


def contract_rows(gains, rows):
    return lax.dot_general(
        gains,
        rows,
        (((0,), (0,)), ((), ())),
        precision=lax.Precision.HIGHEST,
        preferred_element_type=jnp.float32,
    )


def solve_pivot(factor, rhs):
    half = lax.linalg.triangular_solve(factor, rhs, left_side=True, lower=True)
    return lax.linalg.triangular_solve(factor, half, left_side=True, lower=True, transpose_a=True)


def locate(listed, start, count):
    local_ids = listed - start
    valid = (local_ids >= 0) & (local_ids < count)
    clipped = jnp.clip(local_ids, 0, count - 1)
    marked = jnp.zeros((count,), jnp.float32).at[clipped].max(valid.astype(jnp.float32)) > 0.5
    return (clipped, valid, marked)


def per_device(hessian_inverse, weight, pruned):
    row_count = hessian_inverse.shape[0]
    col_count = hessian_inverse.shape[1]
    row_start = lax.axis_index("row") * row_count
    col_start = lax.axis_index("col") * col_count
    inverse = hessian_inverse
    slab = weight.astype(jnp.float32)
    for panel in range(PANELS):
        listed = pruned[panel]
        row_pick, row_valid, row_marked = locate(listed, row_start, row_count)
        col_pick, col_valid, col_marked = locate(listed, col_start, col_count)
        mine_rows = jnp.where(row_valid[:, None], jnp.take(inverse, row_pick, axis=0), 0.0)
        mine_slab = jnp.where(row_valid[:, None], jnp.take(slab, row_pick, axis=0), 0.0)
        panel_rows, slab_rows = lax.psum((mine_rows, mine_slab), "row")
        panel_pivot = jnp.where(col_valid[None, :], jnp.take(panel_rows, col_pick, axis=1), 0.0)
        pivot = lax.psum(panel_pivot, "col")
        factor = jnp.linalg.cholesky(pivot)
        mine_cols = jnp.where(col_valid[None, :], jnp.take(inverse, col_pick, axis=1), 0.0)
        columns = lax.psum(mine_cols, "col")
        gains = solve_pivot(factor, columns.T)
        slab = slab - contract_rows(gains, slab_rows)
        slab = jnp.where(row_marked[:, None], 0.0, slab)
        inverse = inverse - contract_rows(gains, panel_rows)
        inverse = jnp.where(row_marked[:, None] | col_marked[None, :], 0.0, inverse)
    return (inverse, slab.astype(jnp.bfloat16))


def solution(mesh):
    in_specs = (P("row", "col"), P("row", "col"), P())
    out_specs = (P("row", "col"), P("row", "col"))
    return jax.shard_map(
        per_device, mesh=mesh, in_specs=in_specs, out_specs=out_specs, check_vma=False
    )
```

profile of v0, /device:TPU:1, one launch (start us, length us, event | category | flops | bytes accessed | tf_op | source)
XLA Modules:
  0.0 719.2 jit_solution(886581179572580454)
XLA Ops:
  10.1 4.8 gather_fusion
  14.9 2.2 gather_fusion.6
  17.2 1.4 select_select_fusion.1
  19.7 6.0 copy.13
  25.7 6.0 gather_fusion.2
  31.7 2.1 fusion.1
  33.8 53.3 %all-reduce.16.cloned.1.call-done = (f32[512,768]{1,0:T(8,128)}, f32[512,256]{1,0:T(8,128)}) async-done(((f32[512,768]{1,0:T(8,128)}, f32[512,256]{1,0:T(8,128)}), (f32[512,768]{1,0:T(8,128)}, f32[512,256]{1,0:T(8,128)})) %all-reduce.16.cloned.1.call-update) | async-done | bytes 2097168 | tf_op jit(solution)/shard_map/psum | solution.py:45
  87.1 1.9 copy.11
  89.0 1.6 gather_fusion.1
  91.9 4.1 scatter_custom_fusion.3
  96.0 3.7 scatter_custom_fusion.2
  99.8 96.6 %all-reduce.12.cloned.1.call-done = (f32[512,1536]{1,0:T(8,128)}, f32[512,512]{0,1:T(8,128)}) async-done(((f32[512,1536]{1,0:T(8,128)}, f32[512,512]{0,1:T(8,128)}), (f32[512,1536]{1,0:T(8,128)}, f32[512,512]{0,1:T(8,128)})) %all-reduce.12.cloned.1.call-update) | async-done | bytes 4194320 | tf_op jit(solution)/shard_map/psum | solution.py:50
  196.4 1.6 copy.12
  198.3 11.7 %cholesky.286 = f32[128,128]{1,0:T(8,128)S(1)} custom-call(f32[128,128]{1,0:T(8,128)S(1)} %cholesky.426), custom_call_target="Cholesky" | custom-call | tf_op jit(solution)/shard_map/jit(cholesky)/cholesky | solution.py:48
  210.2 9.8 %custom-call.31 = f32[1,128,128]{1,2,0:T(8,128)S(1)} custom-call(f32[1,128,128]{2,1,0:T(8,128)S(1)} %get-tuple-element.100), custom_call_target="InvertDiagBlocksLowerTriangular" | custom-call | tf_op jit(solution)/shard_map/jit(cholesky)/cholesky | solution.py:48
  220.6 11.7 %cholesky.305 = f32[128,128]{1,0:T(8,128)S(1)} custom-call(f32[128,128]{1,0:T(8,128)S(1)} %cholesky.430), custom_call_target="Cholesky" | custom-call | tf_op jit(solution)/shard_map/jit(cholesky)/cholesky | solution.py:48
  232.4 10.2 %custom-call.32 = f32[1,128,128]{1,2,0:T(8,128)S(1)} custom-call(f32[1,128,128]{2,1,0:T(8,128)S(1)} %get-tuple-element.97), custom_call_target="InvertDiagBlocksLowerTriangular" | custom-call | tf_op jit(solution)/shard_map/jit(cholesky)/cholesky | solution.py:48
  243.2 11.7 %cholesky.326 = f32[128,128]{1,0:T(8,128)S(1)} custom-call(f32[128,128]{1,0:T(8,128)S(1)} %cholesky.435), custom_call_target="Cholesky" | custom-call | tf_op jit(solution)/shard_map/jit(cholesky)/cholesky | solution.py:48
  255.0 9.8 %custom-call.33 = f32[1,128,128]{1,2,0:T(8,128)S(1)} custom-call(f32[1,128,128]{2,1,0:T(8,128)S(1)} %get-tuple-element.94), custom_call_target="InvertDiagBlocksLowerTriangular" | custom-call | tf_op jit(solution)/shard_map/jit(cholesky)/cholesky | solution.py:48
  265.4 11.7 %cholesky.343 = f32[128,128]{1,0:T(8,128)S(1)} custom-call(f32[128,128]{1,0:T(8,128)S(1)} %convolution_subtract_fusion.19), custom_call_target="Cholesky" | custom-call | tf_op jit(solution)/shard_map/jit(cholesky)/cholesky | solution.py:48
  282.0 7.6 %while.8 = (s32[]{:T(128)}, f32[512,512]{1,0:T(8,128)S(1)}, s32[4,2]{0,1:T(2,128)S(1)}, f32[4,128,128]{2,1,0:T(8,128)S(1)}, s32[]{:T(128)}) while((s32[]{:T(128)}, f32[512,512]{1,0:T(8,128)S(1)}, s32[4,2]{0,1:T(2,128)S(1)}, f32[4,128,128]{2,1,0:T(8,128)S(1)}, s32[]{:T(128)}) %tuple.80), condition=%wide.while_cond.1, body=%wide.while_body.1.sunk | while | flops 2 | bytes 131189 | solution.py:21
  282.6 1.3 bitcast_dynamic-update-slice_fusion.4
  284.5 1.3 bitcast_dynamic-update-slice_fusion.4
  286.4 1.3 bitcast_dynamic-update-slice_fusion.4
  288.3 1.3 bitcast_dynamic-update-slice_fusion.4
  289.6 39.3 %custom-call.35 = f32[4,128,128]{1,2,0:T(8,128)S(1)} custom-call(f32[4,128,128]{2,1,0:T(8,128)S(1)} %get-tuple-element.38), custom_call_target="InvertDiagBlocksLowerTriangular" | custom-call | tf_op jit(solution)/shard_map/triangular_solve/custom-call.8 | solution.py:21
  328.9 2.0 fusion.41
  330.9 2.1 convolution_subtract_fusion.13
  335.7 1.6 convolution_subtract_fusion.12
  342.4 2.0 convolution_subtract_fusion.10
  345.3 10.7 %subtract_select_fusion.1 = f32[1536,768]{1,0:T(8,128)} fusion(f32[1536,768]{1,0:T(8,128)S(1)} %bitcast.167, f32[512,768]{1,0:T(8,128)S(1)} %copy-done.2, pred[768]{0:T(1024)(128)(4,1)S(1)} %broadcast_compare_fusion.2, pred[1536]{0:T(1024)(128)(4,1)S(1)} %broadcast_compare_fusion, f32[128,1536]{1,0:T(8,128)S(1)} %fusion.83, f32[128,1536]{1,0:T(8,128)S(1)} %fusion.81, ...), kind=kOutput, calls=%fused_computation.17 | convolution fusion | flops 7253655552 | bytes 14158080 | tf_op jit(solution)/shard_map/dot_general | solution.py:10
  356.0 5.5 fusion.3
  361.5 5.4 gather_fusion.3
  366.9 2.2 gather_fusion.7
  369.1 1.4 select_select_fusion
  371.6 6.0 copy.16
  377.7 6.0 gather_fusion.5
  383.7 2.1 fusion
  385.8 50.2 %all-reduce.14.cloned.1.call-done = (f32[512,768]{1,0:T(8,128)}, f32[512,256]{1,0:T(8,128)}) async-done(((f32[512,768]{1,0:T(8,128)}, f32[512,256]{1,0:T(8,128)}), (f32[512,768]{1,0:T(8,128)}, f32[512,256]{1,0:T(8,128)})) %all-reduce.14.cloned.1.call-update) | async-done | bytes 2097168 | tf_op jit(solution)/shard_map/psum | solution.py:45
  436.0 1.9 copy.14
  437.9 1.6 gather_fusion.4
  440.7 4.1 scatter_custom_fusion.1
  444.8 3.7 scatter_custom_fusion
  448.5 96.7 %all-reduce.10.cloned.1.call-done = (f32[512,1536]{1,0:T(8,128)}, f32[512,512]{0,1:T(8,128)}) async-done(((f32[512,1536]{1,0:T(8,128)}, f32[512,512]{0,1:T(8,128)}), (f32[512,1536]{1,0:T(8,128)}, f32[512,512]{0,1:T(8,128)})) %all-reduce.10.cloned.1.call-update) | async-done | bytes 4194320 | tf_op jit(solution)/shard_map/psum | solution.py:50
  545.2 1.6 copy.15
  547.2 11.7 %cholesky.358 = f32[128,128]{1,0:T(8,128)S(1)} custom-call(f32[128,128]{1,0:T(8,128)S(1)} %cholesky.439), custom_call_target="Cholesky" | custom-call | tf_op jit(solution)/shard_map/jit(cholesky)/cholesky | solution.py:48
  559.0 9.8 %custom-call.36 = f32[1,128,128]{1,2,0:T(8,128)S(1)} custom-call(f32[1,128,128]{2,1,0:T(8,128)S(1)} %get-tuple-element.90), custom_call_target="InvertDiagBlocksLowerTriangular" | custom-call | tf_op jit(solution)/shard_map/jit(cholesky)/cholesky | solution.py:48
  569.5 11.7 %cholesky.377 = f32[128,128]{1,0:T(8,128)S(1)} custom-call(f32[128,128]{1,0:T(8,128)S(1)} %cholesky.443), custom_call_target="Cholesky" | custom-call | tf_op jit(solution)/shard_map/jit(cholesky)/cholesky | solution.py:48
  581.3 10.2 %custom-call.37 = f32[1,128,128]{1,2,0:T(8,128)S(1)} custom-call(f32[1,128,128]{2,1,0:T(8,128)S(1)} %get-tuple-element.87), custom_call_target="InvertDiagBlocksLowerTriangular" | custom-call | tf_op jit(solution)/shard_map/jit(cholesky)/cholesky | solution.py:48
  592.1 11.7 %cholesky.398 = f32[128,128]{1,0:T(8,128)S(1)} custom-call(f32[128,128]{1,0:T(8,128)S(1)} %cholesky.448), custom_call_target="Cholesky" | custom-call | tf_op jit(solution)/shard_map/jit(cholesky)/cholesky | solution.py:48
  603.9 9.8 %custom-call.38 = f32[1,128,128]{1,2,0:T(8,128)S(1)} custom-call(f32[1,128,128]{2,1,0:T(8,128)S(1)} %get-tuple-element.84), custom_call_target="InvertDiagBlocksLowerTriangular" | custom-call | tf_op jit(solution)/shard_map/jit(cholesky)/cholesky | solution.py:48
  614.3 11.7 %cholesky.415 = f32[128,128]{1,0:T(8,128)S(1)} custom-call(f32[128,128]{1,0:T(8,128)S(1)} %convolution_subtract_fusion.18), custom_call_target="Cholesky" | custom-call | tf_op jit(solution)/shard_map/jit(cholesky)/cholesky | solution.py:48
  631.7 8.1 %while.9 = (s32[]{:T(128)}, f32[512,512]{1,0:T(8,128)S(1)}, s32[4,2]{0,1:T(2,128)S(1)}, f32[4,128,128]{2,1,0:T(8,128)S(1)}, s32[]{:T(128)}) while((s32[]{:T(128)}, f32[512,512]{1,0:T(8,128)S(1)}, s32[4,2]{0,1:T(2,128)S(1)}, f32[4,128,128]{2,1,0:T(8,128)S(1)}, s32[]{:T(128)}) %tuple.98), condition=%wide.while_cond.1.clone, body=%wide.while_body.1.clone.sunk | while | flops 2 | bytes 131189 | solution.py:21
  632.3 1.4 bitcast_dynamic-update-slice_fusion.5
  634.4 1.4 bitcast_dynamic-update-slice_fusion.5
  636.4 1.4 bitcast_dynamic-update-slice_fusion.5
  638.4 1.4 bitcast_dynamic-update-slice_fusion.5
  639.8 39.3 %custom-call.40 = f32[4,128,128]{1,2,0:T(8,128)S(1)} custom-call(f32[4,128,128]{2,1,0:T(8,128)S(1)} %get-tuple-element.40), custom_call_target="InvertDiagBlocksLowerTriangular" | custom-call | tf_op jit(solution)/shard_map/triangular_solve/custom-call.8 | solution.py:21
  679.1 2.0 fusion.39
  681.1 2.1 convolution_subtract_fusion.9
  685.9 1.6 convolution_subtract_fusion.8
  692.6 1.8 convolution_subtract_fusion.6
  695.3 10.7 %subtract_select_fusion = f32[1536,768]{1,0:T(8,128)} fusion(f32[1536,768]{1,0:T(8,128)S(1)} %bitcast.165, f32[512,768]{1,0:T(8,128)S(1)} %copy-done.3, pred[768]{0:T(1024)(128)(4,1)S(1)} %broadcast_compare_fusion.3, pred[1536]{0:T(1024)(128)(4,1)S(1)} %broadcast_compare_fusion.1, f32[128,1536]{1,0:T(8,128)S(1)} %fusion.90, f32[128,1536]{1,0:T(8,128)S(1)} %fusion.88, ...), kind=kOutput, calls=%fused_computation.16 | convolution fusion | flops 7253655552 | bytes 14158080 | tf_op jit(solution)/shard_map/dot_general | solution.py:10
  705.9 6.5 fusion.4
  (150 shorter events, 39.7 us)
Async XLA Ops:
  7.2 79.9 %all-reduce.16.cloned.1.call-start = ((), (), s32[]{:S(2)}) async-start(), calls=%async_computation.3 | async-start | bytes 4194304 | tf_op jit(solution)/shard_map/psum | solution.py:45
  17.2 1.4 copy-start.8
  19.6 176.8 %all-reduce.12.cloned.1.call-start = ((), (), s32[]{:S(2)}) async-start(), calls=%async_computation.1 | async-start | bytes 8388608 | tf_op jit(solution)/shard_map/psum | solution.py:50
  91.8 344.2 %all-reduce.14.cloned.1.call-start = ((), (), s32[]{:S(2)}) async-start(), calls=%async_computation.2 | async-start | bytes 4194304 | tf_op jit(solution)/shard_map/psum | solution.py:45
  196.4 1.7 copy-start.4
  330.9 2.9 copy-start.6
  338.2 7.0 slice-start.2
  340.6 4.6 slice-start.3
  342.4 2.8 copy-start.2
  345.2 10.7 %copy-start.10 = (bf16[1536,256]{1,0:T(8,128)(2,1)S(1)}, bf16[1536,256]{1,0:T(8,128)(2,1)}, u32[]{:S(2)}) copy-start(bf16[1536,256]{1,0:T(8,128)(2,1)} %param.17) | copy-start | bytes 2359300
  345.3 10.7 %copy-start.11 = (f32[512,256]{1,0:T(8,128)S(1)}, f32[512,256]{1,0:T(8,128)}, u32[]{:S(2)}) copy-start(f32[512,256]{1,0:T(8,128)} %get-tuple-element.68) | copy-start | bytes 1572868
  361.5 5.4 copy-start
  369.1 1.4 copy-start.9
  371.5 173.7 %all-reduce.10.cloned.1.call-start = ((), (), s32[]{:S(2)}) async-start(), calls=%async_computation | async-start | bytes 8388608 | tf_op jit(solution)/shard_map/psum | solution.py:50
  545.2 1.7 copy-start.5
  681.1 2.9 copy-start.7
  688.3 6.9 slice-start
  690.8 4.4 slice-start.1
  692.6 2.6 copy-start.3
  695.2 10.7 %copy-start.1 = (f32[1536,256]{1,0:T(8,128)S(1)}, f32[1536,256]{1,0:T(8,128)}, u32[]{:S(2)}) copy-start(f32[1536,256]{1,0:T(8,128)} %copy-done) | copy-start | bytes 4718596
  695.3 10.7 %copy-start.12 = (f32[512,256]{1,0:T(8,128)S(1)}, f32[512,256]{1,0:T(8,128)}, u32[]{:S(2)}) copy-start(f32[512,256]{1,0:T(8,128)} %get-tuple-element.66) | copy-start | bytes 1572868
Sparse Core Ops, SparseCore 0:
  19.7 67.3 all-reduce.15
  92.0 104.3 all-reduce.11
  371.7 64.2 all-reduce.13
  440.8 104.3 all-reduce.9
where the time goes:
time: 726 us; the launch traced here: 719 us
  waiting for transfers between devices  297 us (41%)
  other arithmetic  268 us (37%)
  matrix products  69.1 us (10%)
  local copies, waits for them, and re-layouts  65 us (9%)
  between operations  20.1 us (3%)
    psum x2, waiting for transfers between devices, per_device(): columns = lax.psum(mine_cols, 'col')  193 us
    another operation x29, other arithmetic, per_device(): factor = jnp.linalg.cholesky(pivot)  158 us
    psum x2, waiting for transfers between devices, per_device(): panel_rows, slab_rows = lax.psum((mine_rows, mine_slab), 'row')  104 us
    another operation x5, other arithmetic, solve_pivot(): lax.linalg.triangular_solve(factor, half, left_side=True, lower=True, tra...  79.2 us
    dot_general x4, matrix products, contract_rows(): lax.dot_general(gains, rows, (((0,), (0,)), ((), ())), precision=lax.Prec...  33.4 us
    another operation x14, matrix products, solve_pivot(): half = lax.linalg.triangular_solve(factor, rhs, left_side=True, lower=True)  18.3 us
    another operation x27, local copies, waits for them, and re-layouts, solve_pivot(): lax.linalg.triangular_solve(factor, half, left_side=True, lower=True, tra...  15.6 us
    another operation x4, other arithmetic, locate(): jnp.zeros((count,), jnp.float32).at[clipped].max(valid.astype(jnp.float32))  15.5 us
  transfers between devices with their start and end apart: 4, of which 4 were waited for; matrix products, arithmetic and copies ran while one was open for 6% of the time, Pallas kernels for 0%

commit v1 on v0

--- a/solution.py
+++ b/solution.py
@@ -47,7 +47,11 @@
         pivot = lax.psum(panel_pivot, "col")
         factor = jnp.linalg.cholesky(pivot)
         mine_cols = jnp.where(col_valid[None, :], jnp.take(inverse, col_pick, axis=1), 0.0)
-        columns = lax.psum(mine_cols, "col")
+        columns = mine_cols
+        for hop in (1, 2, 4, 8):
+            columns = columns + lax.ppermute(
+                columns, "col", [(dev, dev ^ hop) for dev in range(16)]
+            )
         gains = solve_pivot(factor, columns.T)
         slab = slab - contract_rows(gains, slab_rows)
         slab = jnp.where(row_marked[:, None], 0.0, slab)

time: 726 us -> 910 us (1.25)
  waiting for transfers between devices: 297 us -> 414 us
  other arithmetic: 268 us -> 303 us
  starting transfers between devices: 0.16 us -> 13 us
  local copies, waits for them, and re-layouts: 65 us -> 76.5 us
    ppermute x0 -> x8, waiting for transfers between devices: none -> 235 us  [per_device(): lax.ppermute(columns, 'col', [(dev, dev ^ hop) for dev in range(16)])]
    psum x2, waiting for transfers between devices: 104 us -> 19.5 us  [per_device(): panel_rows, slab_rows = lax.psum((mine_rows, mine_slab), 'row')]
    psum x2, waiting for transfers between devices: 193 us -> 160 us  [per_device(): pivot = lax.psum(panel_pivot, 'col')]
    add x0 -> x6, other arithmetic: none -> 21.5 us  [per_device(): columns + lax.ppermute(columns, 'col', [(dev, dev ^ hop) for dev in range...]
    ppermute x0 -> x8, starting transfers between devices: none -> 12.8 us  [per_device(): lax.ppermute(columns, 'col', [(dev, dev ^ hop) for dev in range(16)])]
  transfers between devices with their start and end apart: 4 -> 12, of which waited for: 4 -> 8; matrix products, arithmetic and copies ran while one was open for 6% -> 39% of each run, Pallas kernels for 0% -> 0%
where the time goes in v1:
time: 910 us; the launch traced here: 900 us
  waiting for transfers between devices  414 us (45%)
  other arithmetic  303 us (33%)
  local copies, waits for them, and re-layouts  76.5 us (8%)
  matrix products  71.6 us (8%)
  between operations  20.1 us (2%)
  starting transfers between devices  13 us (1%)
    ppermute x8, waiting for transfers between devices, per_device(): lax.ppermute(columns, 'col', [(dev, dev ^ hop) for dev in range(16)])  235 us
    another operation x29, other arithmetic, per_device(): factor = jnp.linalg.cholesky(pivot)  161 us
    psum x2, waiting for transfers between devices, per_device(): pivot = lax.psum(panel_pivot, 'col')  160 us
    another operation x5, other arithmetic, solve_pivot(): lax.linalg.triangular_solve(factor, half, left_side=True, lower=True, tra...  84.9 us
    dot_general x4, matrix products, contract_rows(): lax.dot_general(gains, rows, (((0,), (0,)), ((), ())), precision=lax.Prec...  34.9 us
    another operation x27, local copies, waits for them, and re-layouts, solve_pivot(): lax.linalg.triangular_solve(factor, half, left_side=True, lower=True, tra...  23.2 us
    add x6, other arithmetic, per_device(): columns + lax.ppermute(columns, 'col', [(dev, dev ^ hop) for dev in range...  21.5 us
    psum x2, waiting for transfers between devices, per_device(): panel_rows, slab_rows = lax.psum((mine_rows, mine_slab), 'row')  19.5 us
  transfers between devices with their start and end apart: 12, of which 8 were waited for; matrix products, arithmetic and copies ran while one was open for 39% of the time, Pallas kernels for 0%

profile of v1, /device:TPU:1, one launch (start us, length us, event | category | flops | bytes accessed | tf_op | source)
XLA Modules:
  0.0 899.6 jit_solution(8846509649391553234)
XLA Ops:
  8.8 6.0 copy.13
  14.9 6.0 gather_fusion.2
  21.3 2.2 collective-permute-start
  23.5 67.5 %collective-permute-done = f32[1536,512]{0,1:T(8,128)S(1)} collective-permute-done((f32[1536,512]{0,1:T(8,128)S(1)}, f32[1536,512]{0,1:T(8,128)S(1)}, u32[]{:S(2)}, u32[]{:S(2)}) %collective-permute-start) | collective-permute-done | bytes 3145760 | tf_op jit(solution)/shard_map/ppermute | solution.py:52
  91.0 2.2 fusion.136
  93.1 3.1 collective-permute-start.1
  96.3 4.8 gather_fusion
  102.4 2.2 gather_fusion.6
  104.6 2.0 select_select_fusion.5
  108.1 55.2 %collective-permute-done.1 = f32[1536,512]{0,1:T(8,128)} collective-permute-done((f32[1536,512]{0,1:T(8,128)}, f32[1536,512]{0,1:T(8,128)}, u32[]{:S(2)}, u32[]{:S(2)}) %collective-permute-start.1) | collective-permute-done | bytes 3145760 | tf_op jit(solution)/shard_map/ppermute | solution.py:52
  163.4 5.1 add.137
  169.6 5.0 all-reduce.14.cloned.1.call-done
  179.5 4.1 scatter_custom_fusion.3
  183.6 3.7 scatter_custom_fusion.2
  187.4 79.9 %all-reduce.8.cloned.1.call-done = f32[512,512]{0,1:T(8,128)} async-done(((f32[512,512]{0,1:T(8,128)}), f32[512,512]{0,1:T(8,128)}) %all-reduce.8.cloned.1.call-update) | async-done | bytes 1048592 | tf_op jit(solution)/shard_map/psum | solution.py:47
  270.3 11.7 %cholesky.286 = f32[128,128]{1,0:T(8,128)S(1)} custom-call(f32[128,128]{1,0:T(8,128)S(1)} %cholesky.426), custom_call_target="Cholesky" | custom-call | tf_op jit(solution)/shard_map/jit(cholesky)/cholesky | solution.py:48
  282.2 9.8 %custom-call.31 = f32[1,128,128]{1,2,0:T(8,128)S(1)} custom-call(f32[1,128,128]{2,1,0:T(8,128)S(1)} %get-tuple-element.96), custom_call_target="InvertDiagBlocksLowerTriangular" | custom-call | tf_op jit(solution)/shard_map/jit(cholesky)/cholesky | solution.py:48
  292.7 11.7 %cholesky.305 = f32[128,128]{1,0:T(8,128)S(1)} custom-call(f32[128,128]{1,0:T(8,128)S(1)} %cholesky.430), custom_call_target="Cholesky" | custom-call | tf_op jit(solution)/shard_map/jit(cholesky)/cholesky | solution.py:48
  304.4 10.2 %custom-call.32 = f32[1,128,128]{1,2,0:T(8,128)S(1)} custom-call(f32[1,128,128]{2,1,0:T(8,128)S(1)} %get-tuple-element.93), custom_call_target="InvertDiagBlocksLowerTriangular" | custom-call | tf_op jit(solution)/shard_map/jit(cholesky)/cholesky | solution.py:48
  314.6 3.4 add.138
  321.3 11.7 %cholesky.326 = f32[128,128]{1,0:T(8,128)S(1)} custom-call(f32[128,128]{1,0:T(8,128)S(1)} %cholesky.435), custom_call_target="Cholesky" | custom-call | tf_op jit(solution)/shard_map/jit(cholesky)/cholesky | solution.py:48
  333.7 9.8 %custom-call.33 = f32[1,128,128]{1,2,0:T(8,128)S(1)} custom-call(f32[1,128,128]{2,1,0:T(8,128)S(1)} %get-tuple-element.90), custom_call_target="InvertDiagBlocksLowerTriangular" | custom-call | tf_op jit(solution)/shard_map/jit(cholesky)/cholesky | solution.py:48
  345.7 11.7 %cholesky.343 = f32[128,128]{1,0:T(8,128)S(1)} custom-call(f32[128,128]{1,0:T(8,128)S(1)} %convolution_subtract_fusion.13), custom_call_target="Cholesky" | custom-call | tf_op jit(solution)/shard_map/jit(cholesky)/cholesky | solution.py:48
  362.5 2.3 select_select_fusion.3
  364.9 12.1 %while.8 = (s32[]{:T(128)}, f32[512,512]{1,0:T(8,128)}, s32[4,2]{0,1:T(2,128)S(1)}, f32[4,128,128]{2,1,0:T(8,128)S(1)}, s32[]{:T(128)}) while((s32[]{:T(128)}, f32[512,512]{1,0:T(8,128)}, s32[4,2]{0,1:T(2,128)S(1)}, f32[4,128,128]{2,1,0:T(8,128)S(1)}, s32[]{:T(128)}) %tuple.80), condition=%wide.while_cond.1, body=%wide.while_body.1.sunk | while | flops 2 | bytes 131189 | solution.py:21
  365.7 2.3 bitcast_dynamic-update-slice_fusion.4
  368.7 2.3 bitcast_dynamic-update-slice_fusion.4
  371.7 2.3 bitcast_dynamic-update-slice_fusion.4
  374.7 2.2 bitcast_dynamic-update-slice_fusion.4
  377.7 40.1 %custom-call.35 = f32[4,128,128]{1,2,0:T(8,128)S(1)} custom-call(f32[4,128,128]{2,1,0:T(8,128)} %copy-done.18), custom_call_target="InvertDiagBlocksLowerTriangular" | custom-call | tf_op jit(solution)/shard_map/triangular_solve/custom-call.8 | solution.py:21
  417.8 2.6 add_bitcast_fusion.1
  434.9 10.7 %subtract_select_fusion.1 = f32[1536,768]{1,0:T(8,128)} fusion(f32[1536,768]{1,0:T(8,128)S(1)} %bitcast.161, f32[512,768]{1,0:T(8,128)S(1)} %copy-done.9, pred[768]{0:T(1024)(128)(4,1)S(1)} %broadcast_compare_fusion.2, pred[1536]{0:T(1024)(128)(4,1)S(1)} %broadcast_compare_fusion, f32[128,1536]{1,0:T(8,128)S(1)} %fusion.90, f32[128,1536]{1,0:T(8,128)S(1)} %fusion.89, ...), kind=kOutput, calls=%fused_computation.17 | convolution fusion | flops 7253655552 | bytes 14158080 | tf_op jit(solution)/shard_map/dot_general | solution.py:10
  445.6 6.0 copy.16
  451.6 6.0 gather_fusion.5
  458.9 65.7 %collective-permute-done.4 = f32[1536,512]{0,1:T(8,128)S(1)} collective-permute-done((f32[1536,512]{0,1:T(8,128)S(1)}, f32[1536,512]{0,1:T(8,128)S(1)}, u32[]{:S(2)}, u32[]{:S(2)}) %collective-permute-start.4) | collective-permute-done | bytes 3145760 | tf_op jit(solution)/shard_map/ppermute | solution.py:52
  524.6 2.2 fusion.135
  526.9 2.3 collective-permute-start.5
  529.2 6.1 gather_fusion.3
  535.3 7.0 fusion.1
  542.3 2.2 gather_fusion.7
  548.1 46.2 %collective-permute-done.5 = f32[1536,512]{0,1:T(8,128)} collective-permute-done((f32[1536,512]{0,1:T(8,128)}, f32[1536,512]{0,1:T(8,128)}, u32[]{:S(2)}, u32[]{:S(2)}) %collective-permute-start.5) | collective-permute-done | bytes 3145760 | tf_op jit(solution)/shard_map/ppermute | solution.py:52
  594.3 5.2 add.141
  600.8 14.5 %all-reduce.12.cloned.1.call-done = (f32[512,768]{1,0:T(8,128)}, f32[512,256]{1,0:T(8,128)}) async-done(((f32[512,768]{1,0:T(8,128)}, f32[512,256]{1,0:T(8,128)}), (f32[512,768]{1,0:T(8,128)}, f32[512,256]{1,0:T(8,128)})) %all-reduce.12.cloned.1.call-update) | async-done | bytes 2097168 | tf_op jit(solution)/shard_map/psum | solution.py:45
  620.0 4.1 scatter_custom_fusion.1
  624.1 3.7 scatter_custom_fusion
  627.8 80.3 %all-reduce.10.cloned.1.call-done = f32[512,512]{0,1:T(8,128)} async-done(((f32[512,512]{0,1:T(8,128)}), f32[512,512]{0,1:T(8,128)}) %all-reduce.10.cloned.1.call-update) | async-done | bytes 1048592 | tf_op jit(solution)/shard_map/psum | solution.py:47
  711.2 11.7 %cholesky.358 = f32[128,128]{1,0:T(8,128)S(1)} custom-call(f32[128,128]{1,0:T(8,128)S(1)} %cholesky.439), custom_call_target="Cholesky" | custom-call | tf_op jit(solution)/shard_map/jit(cholesky)/cholesky | solution.py:48
  723.1 9.8 %custom-call.36 = f32[1,128,128]{1,2,0:T(8,128)S(1)} custom-call(f32[1,128,128]{2,1,0:T(8,128)S(1)} %get-tuple-element.86), custom_call_target="InvertDiagBlocksLowerTriangular" | custom-call | tf_op jit(solution)/shard_map/jit(cholesky)/cholesky | solution.py:48
  733.6 11.7 %cholesky.377 = f32[128,128]{1,0:T(8,128)S(1)} custom-call(f32[128,128]{1,0:T(8,128)S(1)} %cholesky.443), custom_call_target="Cholesky" | custom-call | tf_op jit(solution)/shard_map/jit(cholesky)/cholesky | solution.py:48
  745.3 10.2 %custom-call.37 = f32[1,128,128]{1,2,0:T(8,128)S(1)} custom-call(f32[1,128,128]{2,1,0:T(8,128)S(1)} %get-tuple-element.83), custom_call_target="InvertDiagBlocksLowerTriangular" | custom-call | tf_op jit(solution)/shard_map/jit(cholesky)/cholesky | solution.py:48
  756.8 3.4 add.142
  762.5 11.7 %cholesky.398 = f32[128,128]{1,0:T(8,128)S(1)} custom-call(f32[128,128]{1,0:T(8,128)S(1)} %cholesky.448), custom_call_target="Cholesky" | custom-call | tf_op jit(solution)/shard_map/jit(cholesky)/cholesky | solution.py:48
  774.9 9.8 %custom-call.38 = f32[1,128,128]{1,2,0:T(8,128)S(1)} custom-call(f32[1,128,128]{2,1,0:T(8,128)S(1)} %get-tuple-element.80), custom_call_target="InvertDiagBlocksLowerTriangular" | custom-call | tf_op jit(solution)/shard_map/jit(cholesky)/cholesky | solution.py:48
  787.0 11.7 %cholesky.415 = f32[128,128]{1,0:T(8,128)S(1)} custom-call(f32[128,128]{1,0:T(8,128)S(1)} %convolution_subtract_fusion.12), custom_call_target="Cholesky" | custom-call | tf_op jit(solution)/shard_map/jit(cholesky)/cholesky | solution.py:48
  804.5 2.3 select_select_fusion.2
  806.9 11.6 %while.9 = (s32[]{:T(128)}, f32[512,512]{1,0:T(8,128)}, s32[4,2]{0,1:T(2,128)S(1)}, f32[4,128,128]{2,1,0:T(8,128)S(1)}, s32[]{:T(128)}) while((s32[]{:T(128)}, f32[512,512]{1,0:T(8,128)}, s32[4,2]{0,1:T(2,128)S(1)}, f32[4,128,128]{2,1,0:T(8,128)S(1)}, s32[]{:T(128)}) %tuple.96), condition=%wide.while_cond.1.clone, body=%wide.while_body.1.clone.sunk | while | flops 2 | bytes 131189 | solution.py:21
  807.6 2.3 bitcast_dynamic-update-slice_fusion.5
  810.5 2.3 bitcast_dynamic-update-slice_fusion.5
  813.4 2.3 bitcast_dynamic-update-slice_fusion.5
  816.3 2.2 bitcast_dynamic-update-slice_fusion.5
  819.2 40.1 %custom-call.40 = f32[4,128,128]{1,2,0:T(8,128)S(1)} custom-call(f32[4,128,128]{2,1,0:T(8,128)} %copy-done.17), custom_call_target="InvertDiagBlocksLowerTriangular" | custom-call | tf_op jit(solution)/shard_map/triangular_solve/custom-call.8 | solution.py:21
  859.4 2.6 add_bitcast_fusion
  875.6 10.7 %subtract_select_fusion = f32[1536,768]{1,0:T(8,128)} fusion(f32[1536,768]{1,0:T(8,128)S(1)} %bitcast.159, f32[512,768]{1,0:T(8,128)S(1)} %copy-done.10, pred[768]{0:T(1024)(128)(4,1)S(1)} %broadcast_compare_fusion.3, pred[1536]{0:T(1024)(128)(4,1)S(1)} %broadcast_compare_fusion.1, f32[128,1536]{1,0:T(8,128)S(1)} %fusion.94, f32[128,1536]{1,0:T(8,128)S(1)} %fusion.93, ...), kind=kOutput, calls=%fused_computation.16 | convolution fusion | flops 7253655552 | bytes 14158080 | tf_op jit(solution)/shard_map/dot_general | solution.py:10
  886.3 6.6 fusion.2
  (188 shorter events, 82.0 us)
Async XLA Ops:
  7.2 167.5 %all-reduce.14.cloned.1.call-start = ((), (), s32[]{:S(2)}) async-start(), calls=%async_computation.3 | async-start | bytes 4194304 | tf_op jit(solution)/shard_map/psum | solution.py:45
  21.3 69.7 %collective-permute-start = (f32[1536,512]{0,1:T(8,128)S(1)}, f32[1536,512]{0,1:T(8,128)S(1)}, u32[]{:S(2)}, u32[]{:S(2)}) collective-permute-start(f32[1536,512]{0,1:T(8,128)S(1)} %bitcast_select_fusion.1), channel_id=1, source_target_pairs={{0,1},{1,0},{2,3},{3,2},{4,5},{5,4},{6,7},{7,6},{8,9},{9,8},{10,11... | collective-permute-start | bytes 9437192 | tf_op jit(solution)/shard_map/ppermute | solution.py:52
  93.1 70.2 %collective-permute-start.1 = (f32[1536,512]{0,1:T(8,128)}, f32[1536,512]{0,1:T(8,128)}, u32[]{:S(2)}, u32[]{:S(2)}) collective-permute-start(f32[1536,512]{0,1:T(8,128)} %fusion.136), channel_id=1, source_target_pairs={{0,2},{1,3},{2,0},{3,1},{4,6},{5,7},{6,4},{7,5},{8,10},{9,11},{10,... | collective-permute-start | bytes 9437192 | tf_op jit(solution)/shard_map/ppermute | solution.py:52
  108.1 159.2 %all-reduce.8.cloned.1.call-start = ((), (), s32[]{:S(2)}) async-start(), calls=%async_computation | async-start | bytes 2097152 | tf_op jit(solution)/shard_map/psum | solution.py:47
  168.5 146.1 %collective-permute-start.2 = (f32[1536,512]{0,1:T(8,128)}, f32[1536,512]{0,1:T(8,128)}, u32[]{:S(2)}, u32[]{:S(2)}) collective-permute-start(f32[1536,512]{0,1:T(8,128)} %add.137), channel_id=1, source_target_pairs={{0,4},{1,5},{2,6},{3,7},{4,0},{5,1},{6,2},{7,3},{8,12},{9,13},{10,... | collective-permute-start | bytes 9437192 | tf_op jit(solution)/shard_map/ppermute | solution.py:52
  179.4 435.9 %all-reduce.12.cloned.1.call-start = ((), (), s32[]{:S(2)}) async-start(), calls=%async_computation.2 | async-start | bytes 4194304 | tf_op jit(solution)/shard_map/psum | solution.py:45
  270.3 44.3 %copy-start.15 = (f32[512,512]{1,0:T(8,128)}, f32[512,512]{1,0:T(8,128)S(1)}, u32[]{:S(2)}) copy-start(f32[512,512]{1,0:T(8,128)S(1)} %fusion.40) | copy-start | bytes 3145732
  304.4 10.2 %copy-start.7 = (f32[512,512]{1,0:T(8,128)}, f32[512,512]{1,0:T(8,128)S(1)}, u32[]{:S(2)}) copy-start(f32[512,512]{1,0:T(8,128)S(1)} %get-tuple-element.94) | copy-start | bytes 3145732
  318.1 99.7 %collective-permute-start.3 = (f32[1536,512]{0,1:T(8,128)S(1)}, f32[1536,512]{0,1:T(8,128)}, u32[]{:S(2)}, u32[]{:S(2)}) collective-permute-start(f32[1536,512]{0,1:T(8,128)S(1)} %add.138), channel_id=1, source_target_pairs={{0,8},{1,9},{2,10},{3,11},{4,12},{5,13},{6,14},{7,15},{8,0},{9,1},... | collective-permute-start | bytes 9437192 | tf_op jit(solution)/shard_map/ppermute | solution.py:52
  376.9 0.7 copy-start.18
  417.8 3.4 copy-start.13
  426.3 8.7 slice-start.2
  427.9 6.1 copy-start
  429.6 4.5 copy-start.2
  429.6 5.3 slice-start.3
  431.4 2.6 copy-start.6
  431.4 3.5 copy-start.9
  434.0 0.9 copy-start.14
  458.0 66.6 %collective-permute-start.4 = (f32[1536,512]{0,1:T(8,128)S(1)}, f32[1536,512]{0,1:T(8,128)S(1)}, u32[]{:S(2)}, u32[]{:S(2)}) collective-permute-start(f32[1536,512]{0,1:T(8,128)S(1)} %bitcast_select_fusion), channel_id=1, source_target_pairs={{0,1},{1,0},{2,3},{3,2},{4,5},{5,4},{6,7},{7,6},{8,9},{9,8},{10,11... | collective-permute-start | bytes 9437192 | tf_op jit(solution)/shard_map/ppermute | solution.py:52
  526.9 67.5 %collective-permute-start.5 = (f32[1536,512]{0,1:T(8,128)}, f32[1536,512]{0,1:T(8,128)}, u32[]{:S(2)}, u32[]{:S(2)}) collective-permute-start(f32[1536,512]{0,1:T(8,128)} %fusion.135), channel_id=1, source_target_pairs={{0,2},{1,3},{2,0},{3,1},{4,6},{5,7},{6,4},{7,5},{8,10},{9,11},{10,... | collective-permute-start | bytes 9437192 | tf_op jit(solution)/shard_map/ppermute | solution.py:52
  529.2 6.1 copy-start.1
  529.2 6.1 copy-start.3
  542.3 5.7 copy-start.4
  542.3 4.3 copy-start.11
  548.0 160.1 %all-reduce.10.cloned.1.call-start = ((), (), s32[]{:S(2)}) async-start(), calls=%async_computation.1 | async-start | bytes 2097152 | tf_op jit(solution)/shard_map/psum | solution.py:47
  599.5 157.2 %collective-permute-start.6 = (f32[1536,512]{0,1:T(8,128)}, f32[1536,512]{0,1:T(8,128)}, u32[]{:S(2)}, u32[]{:S(2)}) collective-permute-start(f32[1536,512]{0,1:T(8,128)} %add.141), channel_id=1, source_target_pairs={{0,4},{1,5},{2,6},{3,7},{4,0},{5,1},{6,2},{7,3},{8,12},{9,13},{10,... | collective-permute-start | bytes 9437192 | tf_op jit(solution)/shard_map/ppermute | solution.py:52
  711.2 44.6 %copy-start.16 = (f32[512,512]{1,0:T(8,128)}, f32[512,512]{1,0:T(8,128)S(1)}, u32[]{:S(2)}) copy-start(f32[512,512]{1,0:T(8,128)S(1)} %fusion.39) | copy-start | bytes 3145732
  755.8 1.0 copy-start.8
  760.2 99.2 %collective-permute-start.7 = (f32[1536,512]{0,1:T(8,128)S(1)}, f32[1536,512]{0,1:T(8,128)}, u32[]{:S(2)}, u32[]{:S(2)}) collective-permute-start(f32[1536,512]{0,1:T(8,128)S(1)} %add.142), channel_id=1, source_target_pairs={{0,8},{1,9},{2,10},{3,11},{4,12},{5,13},{6,14},{7,15},{8,0},{9,1},... | collective-permute-start | bytes 9437192 | tf_op jit(solution)/shard_map/ppermute | solution.py:52
  818.5 0.7 copy-start.17
  859.3 3.4 copy-start.12
  867.8 7.7 slice-start
  871.1 4.4 slice-start.1
  872.9 2.6 copy-start.10
  875.6 10.7 %copy-start.5 = (f32[1536,256]{1,0:T(8,128)S(1)}, f32[1536,256]{1,0:T(8,128)}, u32[]{:S(2)}) copy-start(f32[1536,256]{1,0:T(8,128)} %copy-done.4) | copy-start | bytes 4718596
  875.6 10.7 %copy-start.19 = (f32[512,256]{1,0:T(8,128)S(1)}, f32[512,256]{1,0:T(8,128)}, u32[]{:S(2)}) copy-start(f32[512,256]{1,0:T(8,128)} %get-tuple-element.62) | copy-start | bytes 1572868
Sparse Core Ops, SparseCore 0:
  108.2 66.4 all-reduce.13
  179.5 87.7 all-reduce.7
  548.2 67.0 all-reduce.11
  620.1 87.9 all-reduce.9
